TPU v7x, 256 devices: a whole 4x4x8 slice. The times are simulated.
256 devices in a mesh: lead: 16 (over z, core), grp: 16 (over x, y).
Axes of the slice: x: 4, y: 4, z: 8, core: 2. Of those that a mesh axis runs over, the one named last changes fastest.
Arguments:
- matrix_tiles: bfloat16 [512, 384, 384], P(('lead', 'grp')), may hold values from -0.0546875 to 0.0546875
- tile_slot: int32 [16, 32], P('lead'), may hold values from 0 to 31, each once within a row
- tile_cols: int32 [64, 8], P('lead'), may hold values from 0 to 7, as said below
- send_rows: int32 [16, 2, 2], replicated, may hold values from 0 to 3, as said below
- residual: float32 [24576, 128], P(('lead', 'grp')), may hold values from -6 to 6
- diag_inv: float32 [24576], P(('lead', 'grp')), may hold values from 0.25 to 1
Outputs:
- correction: float32 [24576, 128], P(('lead', 'grp'))
Inputs may be any that keep to these rules, and one draw needn't show every extreme that they name: `tile_cols`: entry 0 of every row is that row's own block row within its leader, r for row l * 4 + r; indices below 4 are the leader's own block rows, the next 2 are the rows received from leader l - 1, the last 2 those received from leader l + 1 (cyclic). `send_rows`: the 2 entries of each list are distinct block rows of the sending leader.
All inputs are finite; a program needn't handle non-finite values.
Results may differ from a plain program's by a relative error of at most 0.0013.
Values may be sent and summed in bfloat16 or wider, within the bound.
No kernel may reach another device: no remote copies, remote signals or barrier semaphores. Data moves between devices by JAX's collectives and lax.ppermute only.
A program may use at most 64 MiB of HBM per device.

v0:
```python
import jax
import jax.numpy as jnp
from jax import lax
from jax.sharding import PartitionSpec as P

TILES_ROW = 8
lower_bound = 0.5
upper_bound = 1.5


def from_behind(shard, axis, by):
    devices = lax.axis_size(axis)
    return lax.ppermute(shard, axis, [(i, (i + by) % devices) for i in range(devices)])


def one_sweep(start_residual, inverse, apply_operator):
    center_value = (upper_bound + lower_bound) / 2.0
    half_width = (upper_bound - lower_bound) / 2.0
    ratio_value = center_value / half_width
    update = inverse[:, None] * start_residual / center_value
    approx = update
    rho_now = 1.0 / ratio_value
    rho_next = 1.0 / (2.0 * ratio_value - rho_now)
    remaining = start_residual - apply_operator(approx)
    update = (
        rho_next * rho_now * update + 2.0 * rho_next / half_width * inverse[:, None] * remaining
    )
    approx = approx + update
    return approx


def smooth_twice(rhs_field, inverse, apply_operator):
    first_pass = one_sweep(rhs_field, inverse, apply_operator)
    remaining = rhs_field - apply_operator(first_pass)
    second_pass = one_sweep(remaining, inverse, apply_operator)
    return first_pass + second_pass


def extend(blocks, send_rows):
    position = lax.axis_index("lead")
    mine_up = jnp.take(blocks, send_rows[position, 0], axis=0)
    mine_down = jnp.take(blocks, send_rows[position, 1], axis=0)
    from_lower = from_behind(mine_up, "lead", 1)
    from_upper = from_behind(mine_down, "lead", -1)
    return jnp.concatenate([blocks, from_lower, from_upper], axis=0)


def local(matrix_tiles, tile_slot, tile_cols, send_rows, residual, diag_inv):
    block_rows = tile_cols.shape[0]
    tile_size = matrix_tiles.shape[1]
    member = lax.axis_index("grp")
    share_rows = residual.shape[0]
    group_slots = tile_slot[0]
    group_tiles = lax.all_gather(matrix_tiles, "grp", axis=0, tiled=True)
    full_residual, full_inverse = (
        lax.all_gather(residual, "grp", axis=0, tiled=True),
        lax.all_gather(diag_inv, "grp", axis=0, tiled=True),
    )
    placed = (
        jnp.zeros_like(group_slots)
        .at[group_slots]
        .set(jnp.arange(group_slots.shape[0], dtype=jnp.int32))
    )
    ordered = jnp.take(group_tiles, placed, axis=0)
    ordered = ordered.reshape(block_rows, TILES_ROW, tile_size, tile_size)
    flat_cols = tile_cols.reshape(-1)

    def apply_operator(approx):
        rounded = approx.astype(jnp.bfloat16).reshape(block_rows, tile_size, -1)
        extended = extend(rounded, send_rows)
        operand = jnp.take(extended, flat_cols, axis=0).reshape(
            block_rows, TILES_ROW, tile_size, -1
        )
        coupled = jnp.einsum("rkij,rkjn->rin", ordered, operand, preferred_element_type=jnp.float32)
        return approx / full_inverse[:, None] + coupled.reshape(block_rows * tile_size, -1)

    whole_result = smooth_twice(full_residual, full_inverse, apply_operator)
    correction = lax.dynamic_slice_in_dim(whole_result, member * share_rows, share_rows, 0)
    return correction


def solution(mesh):
    in_specs = (
        P(("lead", "grp"), None, None),
        P("lead", None),
        P("lead", None),
        P(),
        P(("lead", "grp"), None),
        P(("lead", "grp")),
    )
    out_specs = P(("lead", "grp"), None)
    return jax.shard_map(local, mesh=mesh, in_specs=in_specs, out_specs=out_specs, check_vma=False)
```

profile of v0, /device:TPU:97, one launch (start us, length us, event | category | flops | bytes accessed | tf_op | source)
XLA Modules:
  0.0 167.3 jit_solution(6383218233879301720)
XLA Ops:
  6.5 0.7 all-gather.2.cloned.1.call-update
  7.3 1.3 dynamic-slice
  9.2 0.9 dynamic-update-slice
  10.1 0.9 fusion.14
  11.0 34.7 %all-reduce = f32[1536]{0:T(1024)S(1)} all-reduce(f32[1536]{0:T(1024)S(1)} %dynamic-update-slice), channel_id=1, replica_groups=mesh['lead'=16,'grp'=16] {'grp'}, use_global_device_ids=true, to_apply=%add | all-reduce | flops 1536 | bytes 12288
  45.7 21.1 %all_gather.10 = f32[1536,128]{1,0:T(8,128)S(1)} all-gather(f32[96,128]{1,0:T(8,128)} %param.14), channel_id=1, replica_groups=mesh['lead'=16,'grp'=16] {'grp'}, dimensions={0}, use_global_device_ids=true | all-gather | bytes 835584 | tf_op jit(solution)/shard_map/all_gather | solution.py:56
  66.8 0.3 multiply_convert_fusion
  67.1 0.6 gather_fusion.1
  67.7 0.1 broadcast_select_fusion.12
  67.8 13.9 %collective-permute-start = (bf16[2,384,128]{2,1,0:T(8,128)(2,1)S(1)}, bf16[2,384,128]{2,1,0:T(8,128)(2,1)S(1)}, u32[]{:S(2)}, u32[]{:S(2)}) collective-permute-start(bf16[2,384,128]{2,1,0:T(8,128)(2,1)S(1)} %broadcast_select_fusion.12), channel_id=1, source_target_pairs={{0,16},{16,32},{32,48},{48,64},{64,80},{80,96},{96,112},{112,128},... | collective-permute-start | bytes 589832 | tf_op jit(solution)/shard_map/ppermute | solution.py:13
  81.8 0.6 gather_fusion.2
  82.4 0.1 broadcast_select_fusion.9
  82.6 0.7 scatter_custom_fusion
  83.3 0.1 broadcast_in_dim.40
  83.5 0.9 collective-permute-done
  84.4 4.8 %collective-permute-done.1 = bf16[2,384,128]{2,1,0:T(8,128)(2,1)S(1)} collective-permute-done((bf16[2,384,128]{2,1,0:T(8,128)(2,1)S(1)}, bf16[2,384,128]{2,1,0:T(8,128)(2,1)S(1)}, u32[]{:S(2)}, u32[]{:S(2)}) %collective-permute-start.1) | collective-permute-done | bytes 196640 | tf_op jit(solution)/shard_map/ppermute | solution.py:13
  89.2 0.1 pad_maximum_fusion
  89.3 2.6 %gather_fusion.3 = bf16[32,384,128]{2,1,0:T(8,128)(2,1)} fusion(bf16[8,384,128]{2,1,0:T(8,128)(2,1)S(1)} %pad_maximum_fusion, s32[1024]{0:T(1024)S(1)} %pad_clamp_fusion), kind=kCustom, calls=%fused_computation.1.clone | custom fusion | bytes 6291584 | tf_op jit(solution)/shard_map/jit(_take)/gather | solution.py:71
  91.9 3.9 %broadcast_select_fusion.6 = bf16[32,384,128]{2,1,0:T(8,128)(2,1)} fusion(bf16[32,384,128]{2,1,0:T(8,128)(2,1)} %gather_fusion.3, pred[32]{0:T(512)(128)(4,1)S(1)} %compare_and_fusion), kind=kLoop, calls=%fused_computation.20 | loop fusion | flops 1572864 | bytes 6291488 | tf_op jit(solution)/shard_map/jit(_take)/select_n | solution.py:71
  95.9 0.1 all-gather.2.cloned.1.call-done
  96.0 9.8 %gather_fusion = bf16[32,384,384]{2,1,0:T(8,128)(2,1)} fusion(bf16[32,384,384]{2,1,0:T(8,128)(2,1)} %all-gather.2.cloned.1.call-done, s32[1024]{0:T(1024)S(1)} %pad_clamp_fusion.3), kind=kCustom, calls=%fused_computation.9 | custom fusion | bytes 18874496 | tf_op jit(solution)/shard_map/jit(_take)/gather | solution.py:64
  105.7 7.3 %fusion.2 = f32[4,384,128,1]{2,1,3,0:T(8,128)S(1)} fusion(bf16[4,8,384,128]{3,2,1,0:T(8,128)(2,1)} %bitcast.54, bf16[4,8,384,384]{3,2,1,0:T(8,128)(2,1)} %bitcast.42, pred[4,8]{1,0:T(4,128)(4,1)S(1)} %broadcast_in_dim.40), kind=kOutput, calls=%fused_computation.14 | convolution fusion | flops 1212678144 | bytes 13369376 | tf_op jit(solution)/shard_map/rkij,rkjn->rin/dot_general | solution.py:74
  113.0 0.5 fusion.23
  113.5 0.6 gather_fusion.5
  114.1 0.6 gather_fusion.4
  114.7 0.1 broadcast_select_fusion.8
  114.8 0.1 broadcast_select_fusion.11
  114.9 3.2 %collective-permute-start.2 = (bf16[2,384,128]{2,1,0:T(8,128)(2,1)S(1)}, bf16[2,384,128]{2,1,0:T(8,128)(2,1)S(1)}, u32[]{:S(2)}, u32[]{:S(2)}) collective-permute-start(bf16[2,384,128]{2,1,0:T(8,128)(2,1)S(1)} %broadcast_select_fusion.11), channel_id=1, source_target_pairs={{0,16},{16,32},{32,48},{48,64},{64,80},{80,96},{96,112},{112,128},... | collective-permute-start | bytes 589832 | tf_op jit(solution)/shard_map/ppermute | solution.py:13
  118.2 2.6 %collective-permute-done.2 = bf16[2,384,128]{2,1,0:T(8,128)(2,1)S(1)} collective-permute-done((bf16[2,384,128]{2,1,0:T(8,128)(2,1)S(1)}, bf16[2,384,128]{2,1,0:T(8,128)(2,1)S(1)}, u32[]{:S(2)}, u32[]{:S(2)}) %collective-permute-start.2) | collective-permute-done | bytes 196640 | tf_op jit(solution)/shard_map/ppermute | solution.py:13
  120.8 3.7 %collective-permute-done.3 = bf16[2,384,128]{2,1,0:T(8,128)(2,1)S(1)} collective-permute-done((bf16[2,384,128]{2,1,0:T(8,128)(2,1)S(1)}, bf16[2,384,128]{2,1,0:T(8,128)(2,1)S(1)}, u32[]{:S(2)}, u32[]{:S(2)}) %collective-permute-start.3) | collective-permute-done | bytes 196640 | tf_op jit(solution)/shard_map/ppermute | solution.py:13
  124.5 0.1 pad_maximum_fusion.1
  124.6 2.6 %gather_fusion.6 = bf16[32,384,128]{2,1,0:T(8,128)(2,1)} fusion(bf16[8,384,128]{2,1,0:T(8,128)(2,1)S(1)} %pad_maximum_fusion.1, s32[1024]{0:T(1024)S(1)} %pad_clamp_fusion), kind=kCustom, calls=%fused_computation.7.clone | custom fusion | bytes 6291584 | tf_op jit(solution)/shard_map/jit(_take)/gather | solution.py:71
  127.2 2.3 %broadcast_select_fusion.5 = bf16[32,384,128]{2,1,0:T(8,128)(2,1)S(1)} fusion(bf16[32,384,128]{2,1,0:T(8,128)(2,1)} %gather_fusion.6, pred[32]{0:T(512)(128)(4,1)S(1)} %compare_and_fusion), kind=kLoop, calls=%fused_computation.19 | loop fusion | flops 1572864 | bytes 6291488 | tf_op jit(solution)/shard_map/jit(_take)/select_n | solution.py:71
  129.4 6.4 %fusion.1 = f32[4,384,128,1]{2,1,3,0:T(8,128)S(1)} fusion(bf16[4,8,384,128]{3,2,1,0:T(8,128)(2,1)S(1)} %bitcast.56, bf16[4,8,384,384]{3,2,1,0:T(8,128)(2,1)} %bitcast.43, pred[4,8]{1,0:T(4,128)(4,1)S(1)} %broadcast_in_dim.40), kind=kOutput, calls=%fused_computation.13 | convolution fusion | flops 1212678144 | bytes 13369376 | tf_op jit(solution)/shard_map/rkij,rkjn->rin/dot_general | solution.py:74
  135.8 1.3 broadcast_divide_fusion
  137.2 0.7 gather_fusion.8
  137.9 0.7 gather_fusion.7
  138.6 0.7 broadcast_select_fusion.7
  139.3 0.7 broadcast_select_fusion.10
  140.0 0.5 collective-permute-start.5
  140.6 2.0 %collective-permute-done.4 = bf16[2,384,128]{2,1,0:T(8,128)(2,1)S(1)} collective-permute-done((bf16[2,384,128]{2,1,0:T(8,128)(2,1)S(1)}, bf16[2,384,128]{2,1,0:T(8,128)(2,1)S(1)}, u32[]{:S(2)}, u32[]{:S(2)}) %collective-permute-start.4) | collective-permute-done | bytes 196640 | tf_op jit(solution)/shard_map/ppermute | solution.py:13
  142.7 0.7 copy-done
  143.3 3.1 %collective-permute-done.5 = bf16[2,384,128]{2,1,0:T(8,128)(2,1)} collective-permute-done((bf16[2,384,128]{2,1,0:T(8,128)(2,1)S(1)}, bf16[2,384,128]{2,1,0:T(8,128)(2,1)}, u32[]{:S(2)}, u32[]{:S(2)}) %collective-permute-start.5) | collective-permute-done | bytes 196640 | tf_op jit(solution)/shard_map/ppermute | solution.py:13
  146.5 1.1 pad_maximum_fusion.2
  147.6 2.7 %gather_fusion.9 = bf16[32,384,128]{2,1,0:T(8,128)(2,1)} fusion(bf16[8,384,128]{2,1,0:T(8,128)(2,1)S(1)} %pad_maximum_fusion.2, s32[1024]{0:T(1024)} %copy-done.1), kind=kCustom, calls=%fused_computation.8.clone | custom fusion | bytes 6291584 | tf_op jit(solution)/shard_map/jit(_take)/gather | solution.py:71
  150.3 2.3 %broadcast_select_fusion.4 = bf16[32,384,128]{2,1,0:T(8,128)(2,1)S(1)} fusion(bf16[32,384,128]{2,1,0:T(8,128)(2,1)} %gather_fusion.9, pred[32]{0:T(512)(128)(4,1)S(1)} %copy-done.5), kind=kLoop, calls=%fused_computation.18 | loop fusion | flops 1572864 | bytes 6291488 | tf_op jit(solution)/shard_map/jit(_take)/select_n | solution.py:71
  152.6 6.4 %fusion = f32[4,384,128,1]{2,1,3,0:T(8,128)S(1)} fusion(bf16[4,8,384,128]{3,2,1,0:T(8,128)(2,1)S(1)} %bitcast.55, bf16[4,8,384,384]{3,2,1,0:T(8,128)(2,1)} %bitcast.44, pred[4,8]{1,0:T(4,128)(4,1)S(1)} %copy-done.11), kind=kOutput, calls=%fused_computation.12 | convolution fusion | flops 1212678144 | bytes 13369376 | tf_op jit(solution)/shard_map/rkij,rkjn->rin/dot_general | solution.py:74
  159.0 1.5 dynamic-slice_add_fusion
  (46 shorter events, 0.4 us)
Async XLA Ops:
  6.5 76.0 %copy-start.8 = (s32[4,8]{1,0:T(4,128)S(1)}, s32[4,8]{1,0:T(4,128)}, u32[]{:S(2)}) copy-start(s32[4,8]{1,0:T(4,128)} %param.12) | copy-start | bytes 388
  6.5 76.1 %copy-start.9 = (s32[1,32]{1,0:T(1,128)S(1)}, s32[1,32]{1,0:T(1,128)}, u32[]{:S(2)}) copy-start(s32[1,32]{1,0:T(1,128)} %param.11) | copy-start | bytes 388
  6.5 89.4 %all-gather.2.cloned.1.call-start = ((), (), s32[]{:S(2)}) async-start(), calls=%async_computation | async-start | bytes 10027008 | tf_op jit(solution)/shard_map/all_gather | solution.py:54
  45.7 68.5 %copy-start.2 = (s32[1024]{0:T(1024)}, s32[1024]{0:T(1024)S(1)}, u32[]{:S(2)}) copy-start(s32[1024]{0:T(1024)S(1)} %pad_clamp_fusion.2) | copy-start | bytes 12292
  67.7 47.1 %copy-start.6 = (pred[2]{0:T(512)(128)(4,1)}, pred[2]{0:T(512)(128)(4,1)S(1)}, u32[]{:S(2)}) copy-start(pred[2]{0:T(512)(128)(4,1)S(1)} %compare_and_fusion.2) | copy-start | bytes 10
  67.8 16.6 %collective-permute-start = (bf16[2,384,128]{2,1,0:T(8,128)(2,1)S(1)}, bf16[2,384,128]{2,1,0:T(8,128)(2,1)S(1)}, u32[]{:S(2)}, u32[]{:S(2)}) collective-permute-start(bf16[2,384,128]{2,1,0:T(8,128)(2,1)S(1)} %broadcast_select_fusion.12), channel_id=1, source_target_pairs={{0,16},{16,32},{32,48},{48,64},{64,80},{80,96},{96,112},{112,128},... | collective-permute-start | bytes 589832 | tf_op jit(solution)/shard_map/ppermute | solution.py:13
  81.8 31.8 %copy-start.3 = (s32[1024]{0:T(1024)}, s32[1024]{0:T(1024)S(1)}, u32[]{:S(2)}) copy-start(s32[1024]{0:T(1024)S(1)} %pad_clamp_fusion.1) | copy-start | bytes 12292
  82.4 32.3 %copy-start.7 = (pred[2]{0:T(512)(128)(4,1)}, pred[2]{0:T(512)(128)(4,1)S(1)}, u32[]{:S(2)}) copy-start(pred[2]{0:T(512)(128)(4,1)S(1)} %compare_and_fusion.1) | copy-start | bytes 10
  82.5 6.7 %collective-permute-start.1 = (bf16[2,384,128]{2,1,0:T(8,128)(2,1)S(1)}, bf16[2,384,128]{2,1,0:T(8,128)(2,1)S(1)}, u32[]{:S(2)}, u32[]{:S(2)}) collective-permute-start(bf16[2,384,128]{2,1,0:T(8,128)(2,1)S(1)} %broadcast_select_fusion.9), channel_id=1, source_target_pairs={{0,240},{16,0},{32,16},{48,32},{64,48},{80,64},{96,80},{112,96},{1... | collective-permute-start | bytes 589832 | tf_op jit(solution)/shard_map/ppermute | solution.py:13
  83.4 46.0 %copy-start.10 = (pred[4,8]{1,0:T(4,128)(4,1)}, pred[4,8]{1,0:T(4,128)(4,1)S(1)}, u32[]{:S(2)}) copy-start(pred[4,8]{1,0:T(4,128)(4,1)S(1)} %broadcast_in_dim.40) | copy-start | bytes 100
  83.4 41.1 %copy-start.1 = (s32[1024]{0:T(1024)}, s32[1024]{0:T(1024)S(1)}, u32[]{:S(2)}) copy-start(s32[1024]{0:T(1024)S(1)} %pad_clamp_fusion) | copy-start | bytes 12292
  83.5 43.7 %copy-start.4 = (pred[32]{0:T(512)(128)(4,1)}, pred[32]{0:T(512)(128)(4,1)S(1)}, u32[]{:S(2)}) copy-start(pred[32]{0:T(512)(128)(4,1)S(1)} %compare_and_fusion) | copy-start | bytes 100
  114.9 5.8 %collective-permute-start.2 = (bf16[2,384,128]{2,1,0:T(8,128)(2,1)S(1)}, bf16[2,384,128]{2,1,0:T(8,128)(2,1)S(1)}, u32[]{:S(2)}, u32[]{:S(2)}) collective-permute-start(bf16[2,384,128]{2,1,0:T(8,128)(2,1)S(1)} %broadcast_select_fusion.11), channel_id=1, source_target_pairs={{0,16},{16,32},{32,48},{48,64},{64,80},{80,96},{96,112},{112,128},... | collective-permute-start | bytes 589832 | tf_op jit(solution)/shard_map/ppermute | solution.py:13
  118.2 6.3 %collective-permute-start.3 = (bf16[2,384,128]{2,1,0:T(8,128)(2,1)S(1)}, bf16[2,384,128]{2,1,0:T(8,128)(2,1)S(1)}, u32[]{:S(2)}, u32[]{:S(2)}) collective-permute-start(bf16[2,384,128]{2,1,0:T(8,128)(2,1)S(1)} %broadcast_select_fusion.8), channel_id=1, source_target_pairs={{0,240},{16,0},{32,16},{48,32},{64,48},{80,64},{96,80},{112,96},{1... | collective-permute-start | bytes 589832 | tf_op jit(solution)/shard_map/ppermute | solution.py:13
  140.0 2.6 %collective-permute-start.4 = (bf16[2,384,128]{2,1,0:T(8,128)(2,1)S(1)}, bf16[2,384,128]{2,1,0:T(8,128)(2,1)S(1)}, u32[]{:S(2)}, u32[]{:S(2)}) collective-permute-start(bf16[2,384,128]{2,1,0:T(8,128)(2,1)S(1)} %broadcast_select_fusion.10), channel_id=1, source_target_pairs={{0,16},{16,32},{32,48},{48,64},{64,80},{80,96},{96,112},{112,128},... | collective-permute-start | bytes 589832 | tf_op jit(solution)/shard_map/ppermute | solution.py:13
  140.0 6.4 %collective-permute-start.5 = (bf16[2,384,128]{2,1,0:T(8,128)(2,1)S(1)}, bf16[2,384,128]{2,1,0:T(8,128)(2,1)}, u32[]{:S(2)}, u32[]{:S(2)}) collective-permute-start(bf16[2,384,128]{2,1,0:T(8,128)(2,1)S(1)} %broadcast_select_fusion.7), channel_id=1, source_target_pairs={{0,240},{16,0},{32,16},{48,32},{64,48},{80,64},{96,80},{112,96},{1... | collective-permute-start | bytes 589832 | tf_op jit(solution)/shard_map/ppermute | solution.py:13
  142.7 0.7 copy-start
  147.6 2.7 %copy-start.5 = (pred[32]{0:T(512)(128)(4,1)S(1)}, pred[32]{0:T(512)(128)(4,1)}, u32[]{:S(2)}) copy-start(pred[32]{0:T(512)(128)(4,1)} %copy-done.4) | copy-start | bytes 100
  150.3 2.3 %copy-start.11 = (pred[4,8]{1,0:T(4,128)(4,1)S(1)}, pred[4,8]{1,0:T(4,128)(4,1)}, u32[]{:S(2)}) copy-start(pred[4,8]{1,0:T(4,128)(4,1)} %copy-done.10) | copy-start | bytes 100
Sparse Core Ops, SparseCore 0:
  9.8 86.1 all-gather.1
where the time goes:
time: 168 us; the launch traced here: 167 us
  blocking collectives  55.8 us (33%)
  local copies, waits for them, and re-layouts  26.2 us (16%)
  matrix products  20.1 us (12%)
  waiting for transfers between devices  18 us (11%)
  starting transfers between devices  17.7 us (11%)
  other arithmetic  15.2 us (9%)
  between operations  14.4 us (9%)
    unnamed x1, blocking collectives  34.7 us
    all_gather x1, blocking collectives, local(): lax.all_gather(residual, 'grp', axis=0, tiled=True)  21.1 us
    dot_general x3, matrix products, apply_operator(): jnp.einsum('rkij,rkjn->rin', ordered, operand, preferred_element_type=jnp...  20.1 us
    ppermute x6, starting transfers between devices, from_behind(): lax.ppermute(shard, axis, [(i, (i + by) % devices) for i in range(devices)])  17.7 us
    ppermute x6, waiting for transfers between devices, from_behind(): lax.ppermute(shard, axis, [(i, (i + by) % devices) for i in range(devices)])  17.2 us
    gather x1, local copies, waits for them, and re-layouts, local(): ordered = jnp.take(group_tiles, placed, axis=0)  9.76 us
    select_n x4, other arithmetic, apply_operator(): jnp.take(extended, flat_cols, axis=0)  8.43 us
    gather x3, local copies, waits for them, and re-layouts, apply_operator(): jnp.take(extended, flat_cols, axis=0)  7.96 us
  transfers between devices with their start and end apart: 7, of which 7 were waited for; matrix products, arithmetic and copies ran while one was open for 7% of the time, Pallas kernels for 0%

commit v1 on v0

--- a/solution.py
+++ b/solution.py
@@ -53,7 +53,9 @@
     group_slots = tile_slot[0]
     group_tiles = lax.all_gather(matrix_tiles, "grp", axis=0, tiled=True)
     full_residual, full_inverse = (
-        lax.all_gather(residual, "grp", axis=0, tiled=True),
+        jnp.concatenate(
+            lax.all_to_all(jnp.stack([residual] * lax.axis_size("grp")), "grp", 0, 0), axis=0
+        ),
         lax.all_gather(diag_inv, "grp", axis=0, tiled=True),
     )
     placed = (

time: 168 us -> 162 us (0.964)
  blocking collectives: 55.8 us -> 34.4 us
  waiting for transfers between devices: 18 us -> 26.4 us
  starting transfers between devices: 17.7 us -> 21.8 us
  local copies, waits for them, and re-layouts: 26.2 us -> 28.2 us
    all_gather x1 -> x0, blocking collectives: 21.1 us -> none  [local(): lax.all_gather(residual, 'grp', axis=0, tiled=True)]
    all_gather x1, waiting for transfers between devices: 0.12 us -> 10 us  [local(): group_tiles = lax.all_gather(matrix_tiles, 'grp', axis=0, tiled=True)]
    all_to_all x0 -> x1, starting transfers between devices: none -> 6.75 us  [local(): lax.all_to_all(jnp.stack([residual] * lax.axis_size('grp')), 'grp', 0, 0)]
    mul x0 -> x1, other arithmetic: none -> 2.81 us  [one_sweep(): update = inverse[:, None] * start_residual / center_value]
    ppermute x6, starting transfers between devices: 17.7 us -> 15.1 us  [from_behind(): lax.ppermute(shard, axis, [(i, (i + by) % devices) for i in range(devices)])]
    another operation x0 -> x1, local copies, waits for them, and re-layouts: none -> 1.76 us  [local(): jnp.stack([residual] * lax.axis_size('grp'))]
  transfers between devices with their start and end apart: 7 -> 8, of which waited for: 7 -> 6; matrix products, arithmetic and copies ran while one was open for 7% -> 11% of each run, Pallas kernels for 0% -> 0%
where the time goes in v1:
time: 162 us; the launch traced here: 161 us
  blocking collectives  34.4 us (21%)
  local copies, waits for them, and re-layouts  28.2 us (17%)
  waiting for transfers between devices  26.4 us (16%)
  starting transfers between devices  21.8 us (13%)
  matrix products  20 us (12%)
  other arithmetic  15.8 us (10%)
  between operations  14.4 us (9%)
    unnamed x1, blocking collectives  34.4 us
    dot_general x3, matrix products, apply_operator(): jnp.einsum('rkij,rkjn->rin', ordered, operand, preferred_element_type=jnp...  20 us
    ppermute x6, waiting for transfers between devices, from_behind(): lax.ppermute(shard, axis, [(i, (i + by) % devices) for i in range(devices)])  15.6 us
    ppermute x6, starting transfers between devices, from_behind(): lax.ppermute(shard, axis, [(i, (i + by) % devices) for i in range(devices)])  15.1 us
    all_gather x1, waiting for transfers between devices, local(): group_tiles = lax.all_gather(matrix_tiles, 'grp', axis=0, tiled=True)  10 us
    gather x1, local copies, waits for them, and re-layouts, local(): ordered = jnp.take(group_tiles, placed, axis=0)  9.56 us
    select_n x4, other arithmetic, apply_operator(): jnp.take(extended, flat_cols, axis=0)  8.43 us
    gather x3, local copies, waits for them, and re-layouts, apply_operator(): jnp.take(extended, flat_cols, axis=0)  7.79 us
  transfers between devices with their start and end apart: 8, of which 6 were waited for; matrix products, arithmetic and copies ran while one was open for 11% of the time, Pallas kernels for 0%

profile of v1, /device:TPU:97, one launch (start us, length us, event | category | flops | bytes accessed | tf_op | source)
XLA Modules:
  0.0 160.9 jit_solution(15094535875497609346)
XLA Ops:
  6.5 0.7 all-gather.2.cloned.1.call-update
  7.3 1.8 %stack.2 = f32[16,96,128]{2,1,0:T(8,128)} broadcast(f32[96,128]{1,0:T(8,128)} %param.14), dimensions={1,2} | broadcast | bytes 835584 | tf_op jit(solution)/shard_map/stack | solution.py:57
  9.0 6.8 %all-to-all-start = ((f32[16,96,128]{2,1,0:T(8,128)}), f32[16,96,128]{2,1,0:T(8,128)S(1)}, u32[]{:S(2)}, u32[]{:S(2)}) async-start(f32[16,96,128]{2,1,0:T(8,128)} %stack.2), calls=%async_computation | async-start | bytes 1572864 | tf_op jit(solution)/shard_map/all_to_all | solution.py:57
  15.8 0.8 reshape.122
  16.6 0.7 fusion.28
  17.2 0.7 scatter_custom_fusion
  18.0 1.3 dynamic-slice
  19.9 0.9 dynamic-update-slice
  20.8 34.4 %all-reduce = f32[1536]{0:T(1024)S(1)} all-reduce(f32[1536]{0:T(1024)S(1)} %dynamic-update-slice), channel_id=1, replica_groups=mesh['lead'=16,'grp'=16] {'grp'}, use_global_device_ids=true, to_apply=%add | all-reduce | flops 1536 | bytes 12288
  55.2 0.9 fusion.26
  56.3 0.3 fusion.20
  56.5 0.6 gather_fusion.2
  57.1 0.6 gather_fusion.1
  57.8 11.3 %collective-permute-start = (bf16[2,384,128]{2,1,0:T(8,128)(2,1)S(1)}, bf16[2,384,128]{2,1,0:T(8,128)(2,1)S(1)}, u32[]{:S(2)}, u32[]{:S(2)}) collective-permute-start(bf16[2,384,128]{2,1,0:T(8,128)(2,1)S(1)} %broadcast_select_fusion.12), channel_id=1, source_target_pairs={{0,16},{16,32},{32,48},{48,64},{64,80},{80,96},{96,112},{112,128},... | collective-permute-start | bytes 589832 | tf_op jit(solution)/shard_map/ppermute | solution.py:13
  69.2 2.5 %collective-permute-done = bf16[2,384,128]{2,1,0:T(8,128)(2,1)S(1)} collective-permute-done((bf16[2,384,128]{2,1,0:T(8,128)(2,1)S(1)}, bf16[2,384,128]{2,1,0:T(8,128)(2,1)S(1)}, u32[]{:S(2)}, u32[]{:S(2)}) %collective-permute-start) | collective-permute-done | bytes 196640 | tf_op jit(solution)/shard_map/ppermute | solution.py:13
  71.7 4.2 %collective-permute-done.1 = bf16[2,384,128]{2,1,0:T(8,128)(2,1)S(1)} collective-permute-done((bf16[2,384,128]{2,1,0:T(8,128)(2,1)S(1)}, bf16[2,384,128]{2,1,0:T(8,128)(2,1)S(1)}, u32[]{:S(2)}, u32[]{:S(2)}) %collective-permute-start.1) | collective-permute-done | bytes 196640 | tf_op jit(solution)/shard_map/ppermute | solution.py:13
  75.9 0.1 pad_maximum_fusion
  76.0 2.6 %gather_fusion.3 = bf16[32,384,128]{2,1,0:T(8,128)(2,1)} fusion(bf16[8,384,128]{2,1,0:T(8,128)(2,1)S(1)} %pad_maximum_fusion, s32[1024]{0:T(1024)S(1)} %pad_clamp_fusion), kind=kCustom, calls=%fused_computation.1.clone | custom fusion | bytes 6291584 | tf_op jit(solution)/shard_map/jit(_take)/gather | solution.py:73
  78.6 3.9 %broadcast_select_fusion.6 = bf16[32,384,128]{2,1,0:T(8,128)(2,1)} fusion(bf16[32,384,128]{2,1,0:T(8,128)(2,1)} %gather_fusion.3, pred[32]{0:T(512)(128)(4,1)S(1)} %compare_and_fusion), kind=kLoop, calls=%fused_computation.20 | loop fusion | flops 1572864 | bytes 6291488 | tf_op jit(solution)/shard_map/jit(_take)/select_n | solution.py:73
  82.6 10.0 %all-gather.2.cloned.1.call-done = bf16[32,384,384]{2,1,0:T(8,128)(2,1)} async-done(((bf16[2,384,384]{2,1,0:T(8,128)(2,1)}), bf16[32,384,384]{2,1,0:T(8,128)(2,1)}) %all-gather.2.cloned.1.call-update) | async-done | bytes 9437200 | tf_op jit(solution)/shard_map/all_gather | solution.py:54
  92.6 9.6 %gather_fusion = bf16[32,384,384]{2,1,0:T(8,128)(2,1)} fusion(bf16[32,384,384]{2,1,0:T(8,128)(2,1)} %all-gather.2.cloned.1.call-done, s32[1024]{0:T(1024)S(1)} %pad_clamp_fusion.3), kind=kCustom, calls=%fused_computation.9 | custom fusion | bytes 18874496 | tf_op jit(solution)/shard_map/jit(_take)/gather | solution.py:66
  102.1 7.3 %fusion.2 = f32[4,384,128,1]{2,1,3,0:T(8,128)S(1)} fusion(bf16[4,8,384,128]{3,2,1,0:T(8,128)(2,1)} %bitcast.104, bf16[4,8,384,384]{3,2,1,0:T(8,128)(2,1)} %bitcast.101, pred[4,8]{1,0:T(4,128)(4,1)S(1)} %broadcast_in_dim.40), kind=kOutput, calls=%fused_computation.14 | convolution fusion | flops 1212678144 | bytes 13369376 | tf_op jit(solution)/shard_map/rkij,rkjn->rin/dot_general | solution.py:76
  109.4 0.5 fusion.34
  109.9 0.6 gather_fusion.5
  110.5 0.6 gather_fusion.4
  111.1 0.1 broadcast_select_fusion.8
  111.2 0.1 broadcast_select_fusion.11
  111.3 3.2 %collective-permute-start.2 = (bf16[2,384,128]{2,1,0:T(8,128)(2,1)S(1)}, bf16[2,384,128]{2,1,0:T(8,128)(2,1)S(1)}, u32[]{:S(2)}, u32[]{:S(2)}) collective-permute-start(bf16[2,384,128]{2,1,0:T(8,128)(2,1)S(1)} %broadcast_select_fusion.11), channel_id=1, source_target_pairs={{0,16},{16,32},{32,48},{48,64},{64,80},{80,96},{96,112},{112,128},... | collective-permute-start | bytes 589832 | tf_op jit(solution)/shard_map/ppermute | solution.py:13
  114.6 2.5 %collective-permute-done.2 = bf16[2,384,128]{2,1,0:T(8,128)(2,1)S(1)} collective-permute-done((bf16[2,384,128]{2,1,0:T(8,128)(2,1)S(1)}, bf16[2,384,128]{2,1,0:T(8,128)(2,1)S(1)}, u32[]{:S(2)}, u32[]{:S(2)}) %collective-permute-start.2) | collective-permute-done | bytes 196640 | tf_op jit(solution)/shard_map/ppermute | solution.py:13
  117.1 3.7 %collective-permute-done.3 = bf16[2,384,128]{2,1,0:T(8,128)(2,1)S(1)} collective-permute-done((bf16[2,384,128]{2,1,0:T(8,128)(2,1)S(1)}, bf16[2,384,128]{2,1,0:T(8,128)(2,1)S(1)}, u32[]{:S(2)}, u32[]{:S(2)}) %collective-permute-start.3) | collective-permute-done | bytes 196640 | tf_op jit(solution)/shard_map/ppermute | solution.py:13
  120.8 0.1 pad_maximum_fusion.1
  120.9 2.6 %gather_fusion.6 = bf16[32,384,128]{2,1,0:T(8,128)(2,1)} fusion(bf16[8,384,128]{2,1,0:T(8,128)(2,1)S(1)} %pad_maximum_fusion.1, s32[1024]{0:T(1024)S(1)} %pad_clamp_fusion), kind=kCustom, calls=%fused_computation.7.clone | custom fusion | bytes 6291584 | tf_op jit(solution)/shard_map/jit(_take)/gather | solution.py:73
  123.5 2.2 %broadcast_select_fusion.5 = bf16[32,384,128]{2,1,0:T(8,128)(2,1)S(1)} fusion(bf16[32,384,128]{2,1,0:T(8,128)(2,1)} %gather_fusion.6, pred[32]{0:T(512)(128)(4,1)S(1)} %compare_and_fusion), kind=kLoop, calls=%fused_computation.19 | loop fusion | flops 1572864 | bytes 6291488 | tf_op jit(solution)/shard_map/jit(_take)/select_n | solution.py:73
  125.7 6.4 %fusion.1 = f32[4,384,128,1]{2,1,3,0:T(8,128)S(1)} fusion(bf16[4,8,384,128]{3,2,1,0:T(8,128)(2,1)S(1)} %bitcast.106, bf16[4,8,384,384]{3,2,1,0:T(8,128)(2,1)} %bitcast.102, pred[4,8]{1,0:T(4,128)(4,1)S(1)} %broadcast_in_dim.40), kind=kOutput, calls=%fused_computation.13 | convolution fusion | flops 1212678144 | bytes 13369376 | tf_op jit(solution)/shard_map/rkij,rkjn->rin/dot_general | solution.py:76
  132.1 0.9 copy-done
  133.0 0.5 fusion.13
  133.5 0.6 gather_fusion.8
  134.1 0.6 gather_fusion.7
  134.7 0.1 broadcast_select_fusion.7
  134.9 0.5 collective-permute-start.5
  135.4 2.8 %broadcast_multiply_fusion = (f32[1536,128]{1,0:T(8,128)}, f32[1536,128]{1,0:T(8,128)S(1)}, f32[1536,128]{1,0:T(8,128)}) fusion(f32[1536]{0:T(1024)S(1)} %all-reduce, f32[4,384,128,1]{2,1,3,0:T(8,128)} %copy-done, f32[16,96,128]{2,1,0:T(8,128)S(1)} %all-to-all-done, f32[4,384,128,1]{2,1,3,0:T(8,128)S(1)} %fusion.2, f32[1536]{0:T(1024)S(1)} %broadcast_multiply_fusion.1), kind=kLoop, calls=%fused_computation.47 | loop fusion | flops 2359296 | bytes 4730880 | tf_op jit(solution)/shard_map/mul | solution.py:20
  138.2 0.3 broadcast_divide_fusion
  138.5 2.7 %collective-permute-done.5 = bf16[2,384,128]{2,1,0:T(8,128)(2,1)S(1)} collective-permute-done((bf16[2,384,128]{2,1,0:T(8,128)(2,1)S(1)}, bf16[2,384,128]{2,1,0:T(8,128)(2,1)S(1)}, u32[]{:S(2)}, u32[]{:S(2)}) %collective-permute-start.5) | collective-permute-done | bytes 196640 | tf_op jit(solution)/shard_map/ppermute | solution.py:13
  141.2 0.1 pad_maximum_fusion.2
  141.3 2.6 %gather_fusion.9 = bf16[32,384,128]{2,1,0:T(8,128)(2,1)} fusion(bf16[8,384,128]{2,1,0:T(8,128)(2,1)S(1)} %pad_maximum_fusion.2, s32[1024]{0:T(1024)S(1)} %pad_clamp_fusion), kind=kCustom, calls=%fused_computation.8.clone | custom fusion | bytes 6291584 | tf_op jit(solution)/shard_map/jit(_take)/gather | solution.py:73
  143.9 2.2 %broadcast_select_fusion.4 = bf16[32,384,128]{2,1,0:T(8,128)(2,1)S(1)} fusion(bf16[32,384,128]{2,1,0:T(8,128)(2,1)} %gather_fusion.9, pred[32]{0:T(512)(128)(4,1)S(1)} %compare_and_fusion), kind=kLoop, calls=%fused_computation.18 | loop fusion | flops 1572864 | bytes 6291488 | tf_op jit(solution)/shard_map/jit(_take)/select_n | solution.py:73
  146.2 6.4 %fusion = f32[4,384,128,1]{2,1,3,0:T(8,128)S(1)} fusion(bf16[4,8,384,128]{3,2,1,0:T(8,128)(2,1)S(1)} %bitcast.105, bf16[4,8,384,384]{3,2,1,0:T(8,128)(2,1)} %bitcast.103, pred[4,8]{1,0:T(4,128)(4,1)S(1)} %broadcast_in_dim.40), kind=kOutput, calls=%fused_computation.12 | convolution fusion | flops 1212678144 | bytes 13369376 | tf_op jit(solution)/shard_map/rkij,rkjn->rin/dot_general | solution.py:76
  152.5 1.5 dynamic-slice_add_fusion
  (29 shorter events, 0.6 us)
Async XLA Ops:
  6.5 86.0 %all-gather.2.cloned.1.call-start = ((), (), s32[]{:S(2)}) async-start(), calls=%async_computation.1 | async-start | bytes 10027008 | tf_op jit(solution)/shard_map/all_gather | solution.py:54
  9.0 47.2 %all-to-all-start = ((f32[16,96,128]{2,1,0:T(8,128)}), f32[16,96,128]{2,1,0:T(8,128)S(1)}, u32[]{:S(2)}, u32[]{:S(2)}) async-start(f32[16,96,128]{2,1,0:T(8,128)} %stack.2), calls=%async_computation | async-start | bytes 1572864 | tf_op jit(solution)/shard_map/all_to_all | solution.py:57
  57.8 13.9 %collective-permute-start = (bf16[2,384,128]{2,1,0:T(8,128)(2,1)S(1)}, bf16[2,384,128]{2,1,0:T(8,128)(2,1)S(1)}, u32[]{:S(2)}, u32[]{:S(2)}) collective-permute-start(bf16[2,384,128]{2,1,0:T(8,128)(2,1)S(1)} %broadcast_select_fusion.12), channel_id=1, source_target_pairs={{0,16},{16,32},{32,48},{48,64},{64,80},{80,96},{96,112},{112,128},... | collective-permute-start | bytes 589832 | tf_op jit(solution)/shard_map/ppermute | solution.py:13
  69.2 6.7 %collective-permute-start.1 = (bf16[2,384,128]{2,1,0:T(8,128)(2,1)S(1)}, bf16[2,384,128]{2,1,0:T(8,128)(2,1)S(1)}, u32[]{:S(2)}, u32[]{:S(2)}) collective-permute-start(bf16[2,384,128]{2,1,0:T(8,128)(2,1)S(1)} %broadcast_select_fusion.9), channel_id=1, source_target_pairs={{0,240},{16,0},{32,16},{48,32},{64,48},{80,64},{96,80},{112,96},{1... | collective-permute-start | bytes 589832 | tf_op jit(solution)/shard_map/ppermute | solution.py:13
  111.3 5.8 %collective-permute-start.2 = (bf16[2,384,128]{2,1,0:T(8,128)(2,1)S(1)}, bf16[2,384,128]{2,1,0:T(8,128)(2,1)S(1)}, u32[]{:S(2)}, u32[]{:S(2)}) collective-permute-start(bf16[2,384,128]{2,1,0:T(8,128)(2,1)S(1)} %broadcast_select_fusion.11), channel_id=1, source_target_pairs={{0,16},{16,32},{32,48},{48,64},{64,80},{80,96},{96,112},{112,128},... | collective-permute-start | bytes 589832 | tf_op jit(solution)/shard_map/ppermute | solution.py:13
  114.5 6.3 %collective-permute-start.3 = (bf16[2,384,128]{2,1,0:T(8,128)(2,1)S(1)}, bf16[2,384,128]{2,1,0:T(8,128)(2,1)S(1)}, u32[]{:S(2)}, u32[]{:S(2)}) collective-permute-start(bf16[2,384,128]{2,1,0:T(8,128)(2,1)S(1)} %broadcast_select_fusion.8), channel_id=1, source_target_pairs={{0,240},{16,0},{32,16},{48,32},{64,48},{80,64},{96,80},{112,96},{1... | collective-permute-start | bytes 589832 | tf_op jit(solution)/shard_map/ppermute | solution.py:13
  132.1 0.9 copy-start
  134.9 3.6 %collective-permute-start.4 = (bf16[2,384,128]{2,1,0:T(8,128)(2,1)S(1)}, bf16[2,384,128]{2,1,0:T(8,128)(2,1)S(1)}, u32[]{:S(2)}, u32[]{:S(2)}) collective-permute-start(bf16[2,384,128]{2,1,0:T(8,128)(2,1)S(1)} %broadcast_select_fusion.10), channel_id=1, source_target_pairs={{0,16},{16,32},{32,48},{48,64},{64,80},{80,96},{96,112},{112,128},... | collective-permute-start | bytes 589832 | tf_op jit(solution)/shard_map/ppermute | solution.py:13
  134.9 6.3 %collective-permute-start.5 = (bf16[2,384,128]{2,1,0:T(8,128)(2,1)S(1)}, bf16[2,384,128]{2,1,0:T(8,128)(2,1)S(1)}, u32[]{:S(2)}, u32[]{:S(2)}) collective-permute-start(bf16[2,384,128]{2,1,0:T(8,128)(2,1)S(1)} %broadcast_select_fusion.7), channel_id=1, source_target_pairs={{0,240},{16,0},{32,16},{48,32},{64,48},{80,64},{96,80},{112,96},{1... | collective-permute-start | bytes 589832 | tf_op jit(solution)/shard_map/ppermute | solution.py:13
Sparse Core Ops, SparseCore 0:
  9.8 82.7 all-gather.1
